TPU v7x, 32 devices: a whole 2x2x4 slice. The times are simulated.
32 devices in a mesh: dp: 8 (over z, x), tensor: 4 (over y, core).
Axes of the slice: x: 2, y: 2, z: 4, core: 2. Of those that a mesh axis runs over, the one named last changes fastest.
Arguments:
- inputs: bfloat16 [2, 8, 1024, 1152], P(None, 'dp', 'tensor'), may hold values from -6 to 6
- lengths: int32 [2, 8], P(None, 'dp'), may hold values from 256 to 1024, as said below
- gain_attn: bfloat16 [1152], P('dp'), may hold values from 0.5 to 1.5
- gain_mlp: bfloat16 [1152], P('dp'), may hold values from 0.5 to 1.5
- w_query: bfloat16 [1152, 1152], P('dp'), may hold values from -0.1875 to 0.1875
- key_weight: bfloat16 [1152, 384], P('dp'), may hold values from -0.1875 to 0.1875
- value_weight: bfloat16 [1152, 384], P('dp'), may hold values from -0.1875 to 0.1875
- w_gate: bfloat16 [1152, 3072], P('dp', 'tensor'), may hold values from -0.1875 to 0.1875
- w_up: bfloat16 [1152, 3072], P('dp', 'tensor'), may hold values from -0.1875 to 0.1875
- w_out: bfloat16 [1152, 1152], P('dp'), may hold values from -0.75 to 0.75
- w_down: bfloat16 [3072, 1152], P('tensor', 'dp'), may hold values from -0.21875 to 0.21875
- cotangent: bfloat16 [2, 8, 1024, 1152], P(None, 'dp', 'tensor'), may hold values from -6 to 6
Outputs:
- out_act: bfloat16 [2, 8, 1024, 1152], P(None, 'dp', 'tensor')
- grad_inputs: bfloat16 [2, 8, 1024, 1152], P(None, 'dp', 'tensor')
- grad_gain_attn: float32 [1152], P('dp')
- grad_gain_mlp: float32 [1152], P('dp')
- grad_w_query: float32 [1152, 1152], P('dp')
- grad_w_key: float32 [1152, 384], P('dp')
- grad_w_value: float32 [1152, 384], P('dp')
- grad_w_gate: float32 [1152, 3072], P('dp', 'tensor')
- grad_w_up: float32 [1152, 3072], P('dp', 'tensor')
- grad_w_out: float32 [1152, 1152], P('dp')
- grad_w_down: float32 [3072, 1152], P('tensor', 'dp')
Inputs may be any that keep to these rules, and one draw needn't show every extreme that they name: `lengths`: each sequence's valid tokens; in every micro-batch one sequence fills all 1024 slots.
All inputs are finite; a program needn't handle non-finite values.
Results may differ from a plain program's by a relative error of at most 0.023.
Values may be sent and summed in bfloat16 or wider, within the bound.
No kernel may reach another device: no remote copies, remote signals or barrier semaphores. Data moves between devices by JAX's collectives and lax.ppermute only.
A program may use at most 192 MiB of HBM per device.

v0:
```python
import jax
import jax.numpy as jnp
from jax import lax
from jax.sharding import PartitionSpec as P

HEAD_SIZE = 64
EPSILON = 1e-05
ROPE_BASE = 10000.0
MASKED = -1e30


def rope_tables(positions, head_dim):
    half_dim = head_dim // 2
    exponent = jnp.arange(half_dim, dtype=jnp.float32) * (2.0 / head_dim)
    frequency = ROPE_BASE ** (-exponent)
    angles = positions[:, None] * frequency[None, :]
    cosine_table = jnp.concatenate([jnp.cos(angles), jnp.cos(angles)], axis=1)
    sine_table = jnp.concatenate([jnp.sin(angles), jnp.sin(angles)], axis=1)
    return (cosine_table, sine_table)


def rotate_half(values):
    half_dim = values.shape[-1] // 2
    return jnp.concatenate([-values[..., half_dim:], values[..., :half_dim]], axis=-1)


def apply_rotary(values, cosine_table, sine_table):
    return values * cosine_table[:, None, :] + rotate_half(values) * sine_table[:, None, :]


def unrope(grads_in, cosine_table, sine_table):
    half_dim = grads_in.shape[-1] // 2
    scaled = grads_in * sine_table[:, None, :]
    turned = jnp.concatenate([scaled[..., half_dim:], -scaled[..., :half_dim]], axis=-1)
    return grads_in * cosine_table[:, None, :] + turned


def contract_rows(left_side, right_side):
    return lax.dot_general(
        left_side, right_side, (((0,), (0,)), ((), ())), preferred_element_type=jnp.float32
    )


def contract_last(left_side, right_side):
    return lax.dot_general(
        left_side, right_side, (((1,), (1,)), ((), ())), preferred_element_type=jnp.float32
    )


def fetch_weights(
    gain_attn, gain_mlp, w_query, key_weight, value_weight, w_gate, w_up, w_out, w_down
):
    return (
        lax.all_gather(gain_attn, "dp", axis=0, tiled=True),
        lax.all_gather(gain_mlp, "dp", axis=0, tiled=True),
        lax.all_gather(w_query, "dp", axis=0, tiled=True),
        lax.all_gather(key_weight, "dp", axis=0, tiled=True),
        lax.all_gather(value_weight, "dp", axis=0, tiled=True),
        lax.all_gather(w_gate, "dp", axis=0, tiled=True),
        lax.all_gather(w_up, "dp", axis=0, tiled=True),
        lax.all_gather(w_out, "dp", axis=0, tiled=True),
        lax.all_gather(w_down, "dp", axis=1, tiled=True),
    )


def project_sum(left_side, right_side):
    return lax.psum_scatter(
        jnp.dot(left_side, right_side, preferred_element_type=jnp.float32).astype(jnp.bfloat16),
        "tensor",
        scatter_dimension=0,
        tiled=True,
    ).astype(jnp.float32)


def back_project_sum(pair_list):
    row_share = pair_list[0][0].shape[0] // lax.axis_size("tensor")
    out_width = pair_list[0][1].shape[0]
    summed = jnp.zeros((lax.axis_size("tensor") * row_share, out_width), jnp.float32)
    for grad_part, weight_part in pair_list:
        summed = summed + contract_last(grad_part, weight_part)
    return lax.psum_scatter(
        summed.astype(jnp.bfloat16), "tensor", scatter_dimension=0, tiled=True
    ).astype(jnp.float32)


def reduce_over_data(grad_list):
    (
        grad_query_w,
        grad_key_w,
        grad_value_w,
        grad_gate_w,
        grad_up_w,
        grad_out_w,
        grad_down_w,
        grad_gain_one,
        grad_gain_two,
    ) = grad_list
    return (
        lax.psum_scatter(grad_query_w, "dp", scatter_dimension=0, tiled=True),
        lax.psum_scatter(grad_key_w, "dp", scatter_dimension=0, tiled=True),
        lax.psum_scatter(grad_value_w, "dp", scatter_dimension=0, tiled=True),
        lax.psum_scatter(grad_gate_w, "dp", scatter_dimension=0, tiled=True),
        lax.psum_scatter(grad_up_w, "dp", scatter_dimension=0, tiled=True),
        lax.psum_scatter(grad_out_w, "dp", scatter_dimension=0, tiled=True),
        lax.psum_scatter(grad_down_w, "dp", scatter_dimension=1, tiled=True),
        lax.psum_scatter(grad_gain_one, "dp", scatter_dimension=0, tiled=True),
        lax.psum_scatter(grad_gain_two, "dp", scatter_dimension=0, tiled=True),
    )


def row_scale_of(values):
    return lax.rsqrt(jnp.mean(values * values, axis=-1, keepdims=True) + EPSILON)


def make_mask(query_pos, position_count, valid_count):
    key_pos = jnp.arange(position_count, dtype=jnp.int32)
    return (key_pos[None, :] <= query_pos[:, None]) & (key_pos[None, :] < valid_count)


def attention_scores(query_rows, keys_all, allowed):
    raw_scores = jnp.einsum(
        "qhgd,shd->hgqs", query_rows, keys_all, preferred_element_type=jnp.float32
    ) * HEAD_SIZE ** (-0.5)
    return jnp.where(allowed, raw_scores, MASKED)


def norm_backward(grad_normed, row_values, row_scale, gain_full):
    gain_grad = jnp.sum(grad_normed * row_values * row_scale, axis=0)
    inner_grad = grad_normed * gain_full
    row_grad = row_scale * inner_grad - row_values * row_scale**3 * jnp.mean(
        inner_grad * row_values, axis=-1, keepdims=True
    )
    return (row_grad, gain_grad)


def forward_pass(rows_in, valid_count, weights, row_start):
    (
        gain_attn,
        gain_mlp,
        full_query,
        full_key,
        full_value,
        full_gate,
        full_up,
        full_out,
        full_down,
    ) = weights
    gain_one = gain_attn.astype(jnp.float32)
    gain_two = gain_mlp.astype(jnp.float32)
    row_count = rows_in.shape[0]
    row_values = rows_in.astype(jnp.float32)
    scale_one = row_scale_of(row_values)
    hidden_one = (row_values * scale_one * gain_one).astype(jnp.bfloat16)
    query_heads = full_query.shape[1] // HEAD_SIZE
    key_heads = full_key.shape[1] // HEAD_SIZE
    group_width = query_heads // key_heads
    query_pos = row_start + jnp.arange(row_count, dtype=jnp.int32)
    cosine_table, sine_table = rope_tables(query_pos.astype(jnp.float32), HEAD_SIZE)
    query_unrotated = jnp.dot(hidden_one, full_query, preferred_element_type=jnp.float32).reshape(
        row_count, query_heads, HEAD_SIZE
    )
    key_unrotated = jnp.dot(hidden_one, full_key, preferred_element_type=jnp.float32).reshape(
        row_count, key_heads, HEAD_SIZE
    )
    values_own = jnp.dot(hidden_one, full_value, preferred_element_type=jnp.float32).astype(
        jnp.bfloat16
    )
    query_rows = (
        apply_rotary(query_unrotated, cosine_table, sine_table)
        .astype(jnp.bfloat16)
        .reshape(row_count, key_heads, group_width, HEAD_SIZE)
    )
    keys_own = (
        apply_rotary(key_unrotated, cosine_table, sine_table)
        .astype(jnp.bfloat16)
        .reshape(row_count, key_heads * HEAD_SIZE)
    )
    keys_flat, values_flat = (
        lax.all_gather(keys_own, "tensor", axis=0, tiled=True),
        lax.all_gather(values_own, "tensor", axis=0, tiled=True),
    )
    position_count = keys_flat.shape[0]
    keys_all = keys_flat.reshape(position_count, key_heads, HEAD_SIZE)
    values_all = values_flat.reshape(position_count, key_heads, HEAD_SIZE)
    allowed = make_mask(query_pos, position_count, valid_count)
    scores = attention_scores(query_rows, keys_all, allowed)
    maxima = jnp.max(scores, axis=-1, keepdims=True)
    log_total = maxima + jnp.log(jnp.sum(jnp.exp(scores - maxima), axis=-1, keepdims=True))
    soft_low = jnp.exp(scores - log_total).astype(jnp.bfloat16)
    attended = jnp.einsum(
        "hgqs,shd->qhgd", soft_low, values_all, preferred_element_type=jnp.float32
    )
    attended = attended.reshape(row_count, query_heads * HEAD_SIZE).astype(jnp.bfloat16)
    middle = row_values + jnp.dot(attended, full_out, preferred_element_type=jnp.float32)
    scale_two = row_scale_of(middle)
    hidden_two = lax.all_gather(
        (middle * scale_two * gain_two).astype(jnp.bfloat16), "tensor", axis=0, tiled=True
    )
    gate_proj = jnp.dot(hidden_two, full_gate, preferred_element_type=jnp.float32)
    up_proj = jnp.dot(hidden_two, full_up, preferred_element_type=jnp.float32)
    activated = (jax.nn.silu(gate_proj) * up_proj).astype(jnp.bfloat16)
    ffn_out = project_sum(activated, full_down)
    valid = (query_pos < valid_count).astype(jnp.float32)[:, None]
    output = (valid * (middle + ffn_out)).astype(jnp.bfloat16)
    kept = (
        row_values,
        scale_one,
        hidden_one,
        query_rows,
        keys_all,
        values_all,
        allowed,
        log_total,
        attended,
        middle,
        scale_two,
        hidden_two,
        gate_proj,
        up_proj,
        activated,
        valid,
        cosine_table,
        sine_table,
    )
    return (output, kept)


def backward_pass(cot_rows, weights, kept):
    (
        gain_attn,
        gain_mlp,
        full_query,
        full_key,
        full_value,
        full_gate,
        full_up,
        full_out,
        full_down,
    ) = weights
    (
        row_values,
        scale_one,
        hidden_one,
        query_rows,
        keys_all,
        values_all,
        allowed,
        log_total,
        attended,
        middle,
        scale_two,
        hidden_two,
        gate_proj,
        up_proj,
        activated,
        valid,
        cosine_table,
        sine_table,
    ) = kept
    gain_one = gain_attn.astype(jnp.float32)
    gain_two = gain_mlp.astype(jnp.float32)
    row_count = row_values.shape[0]
    position_count = keys_all.shape[0]
    query_heads = full_query.shape[1] // HEAD_SIZE
    key_heads = full_key.shape[1] // HEAD_SIZE
    group_width = query_heads // key_heads
    grad_rows = cot_rows.astype(jnp.float32) * valid
    grad_ffn = lax.all_gather(grad_rows.astype(jnp.bfloat16), "tensor", axis=0, tiled=True)
    grad_down_w = contract_rows(activated, grad_ffn)
    grad_act = contract_last(grad_ffn, full_down)
    sigmoid_gate = jax.nn.sigmoid(gate_proj)
    grad_gate = (
        grad_act * up_proj * sigmoid_gate * (1.0 + gate_proj * (1.0 - sigmoid_gate))
    ).astype(jnp.bfloat16)
    grad_up = (grad_act * gate_proj * sigmoid_gate).astype(jnp.bfloat16)
    grad_gate_w = contract_rows(hidden_two, grad_gate)
    grad_up_w = contract_rows(hidden_two, grad_up)
    grad_normed_two = back_project_sum(((grad_gate, full_gate), (grad_up, full_up)))
    row_grad_two, grad_gain_two = norm_backward(grad_normed_two, middle, scale_two, gain_two)
    grad_middle = grad_rows + row_grad_two
    grad_branch = grad_middle.astype(jnp.bfloat16)
    grad_out_w = contract_rows(attended, grad_branch)
    grad_att = (
        contract_last(grad_branch, full_out)
        .astype(jnp.bfloat16)
        .reshape(row_count, key_heads, group_width, HEAD_SIZE)
    )
    soft_float = jnp.exp(attention_scores(query_rows, keys_all, allowed) - log_total)
    grad_soft = jnp.einsum(
        "qhgd,shd->hgqs", grad_att, values_all, preferred_element_type=jnp.float32
    )
    grad_scores = (
        soft_float * (grad_soft - jnp.sum(soft_float * grad_soft, axis=-1, keepdims=True))
    ).astype(jnp.bfloat16)
    value_part = jnp.einsum(
        "hgqs,qhgd->shd",
        soft_float.astype(jnp.bfloat16),
        grad_att,
        preferred_element_type=jnp.float32,
    )
    score_scale = HEAD_SIZE ** (-0.5)
    key_part = (
        jnp.einsum("hgqs,qhgd->shd", grad_scores, query_rows, preferred_element_type=jnp.float32)
        * score_scale
    )
    grad_queries = (
        jnp.einsum("hgqs,shd->qhgd", grad_scores, keys_all, preferred_element_type=jnp.float32)
        * score_scale
    )
    grad_queries = (
        unrope(grad_queries.reshape(row_count, query_heads, HEAD_SIZE), cosine_table, sine_table)
        .astype(jnp.bfloat16)
        .reshape(row_count, query_heads * HEAD_SIZE)
    )
    key_own, value_own = (
        lax.psum_scatter(
            key_part.reshape(position_count, key_heads * HEAD_SIZE).astype(jnp.bfloat16),
            "tensor",
            scatter_dimension=0,
            tiled=True,
        ).astype(jnp.float32),
        lax.psum_scatter(
            value_part.reshape(position_count, key_heads * HEAD_SIZE).astype(jnp.bfloat16),
            "tensor",
            scatter_dimension=0,
            tiled=True,
        ).astype(jnp.float32),
    )
    grad_keys = (
        unrope(key_own.reshape(row_count, key_heads, HEAD_SIZE), cosine_table, sine_table)
        .astype(jnp.bfloat16)
        .reshape(row_count, key_heads * HEAD_SIZE)
    )
    grad_values = value_own.astype(jnp.bfloat16)
    grad_query_w = contract_rows(hidden_one, grad_queries)
    grad_key_w = contract_rows(hidden_one, grad_keys)
    grad_value_w = contract_rows(hidden_one, grad_values)
    grad_normed_one = (
        contract_last(grad_queries, full_query)
        + contract_last(grad_keys, full_key)
        + contract_last(grad_values, full_value)
    )
    row_grad_one, grad_gain_one = norm_backward(grad_normed_one, row_values, scale_one, gain_one)
    grad_input = (grad_middle + row_grad_one).astype(jnp.bfloat16)
    return (
        grad_input,
        (
            grad_query_w,
            grad_key_w,
            grad_value_w,
            grad_gate_w,
            grad_up_w,
            grad_out_w,
            grad_down_w,
            grad_gain_one,
            grad_gain_two,
        ),
    )


def shards(
    inputs,
    lengths,
    gain_attn,
    gain_mlp,
    w_query,
    key_weight,
    value_weight,
    w_gate,
    w_up,
    w_out,
    w_down,
    cotangent,
):
    micro_count = inputs.shape[0]
    row_share = inputs.shape[2]
    row_start = lax.axis_index("tensor") * row_share
    outputs = []
    input_grads = []
    grad_totals = None
    for batch_index in range(micro_count):
        current = fetch_weights(
            gain_attn, gain_mlp, w_query, key_weight, value_weight, w_gate, w_up, w_out, w_down
        )
        output, kept = forward_pass(
            inputs[batch_index, 0], lengths[batch_index, 0], current, row_start
        )
        grad_input, batch_grads = backward_pass(cotangent[batch_index, 0], current, kept)
        if batch_index == 0:
            grad_totals = batch_grads
        else:
            grad_totals = jax.tree.map(jnp.add, grad_totals, batch_grads)
        outputs.append(output)
        input_grads.append(grad_input)
    grad_totals = reduce_over_data(grad_totals)
    (
        grad_query_w,
        grad_key_w,
        grad_value_w,
        grad_gate_w,
        grad_up_w,
        grad_out_w,
        grad_down_w,
        grad_gain_one,
        grad_gain_two,
    ) = grad_totals
    grad_query_w, grad_key_w, grad_value_w, grad_out_w, grad_gain_one, grad_gain_two = (
        lax.psum(grad_query_w.astype(jnp.bfloat16), "tensor").astype(jnp.float32),
        lax.psum(grad_key_w.astype(jnp.bfloat16), "tensor").astype(jnp.float32),
        lax.psum(grad_value_w.astype(jnp.bfloat16), "tensor").astype(jnp.float32),
        lax.psum(grad_out_w.astype(jnp.bfloat16), "tensor").astype(jnp.float32),
        lax.psum(grad_gain_one.astype(jnp.bfloat16), "tensor").astype(jnp.float32),
        lax.psum(grad_gain_two.astype(jnp.bfloat16), "tensor").astype(jnp.float32),
    )
    out_stack = jnp.stack(outputs)[:, None]
    grad_stack = jnp.stack(input_grads)[:, None]
    return (
        out_stack,
        grad_stack,
        grad_gain_one,
        grad_gain_two,
        grad_query_w,
        grad_key_w,
        grad_value_w,
        grad_gate_w,
        grad_up_w,
        grad_out_w,
        grad_down_w,
    )


def solution(mesh):
    in_specs = (
        P(None, "dp", "tensor", None),
        P(None, "dp"),
        P("dp"),
        P("dp"),
        P("dp", None),
        P("dp", None),
        P("dp", None),
        P("dp", "tensor"),
        P("dp", "tensor"),
        P("dp", None),
        P("tensor", "dp"),
        P(None, "dp", "tensor", None),
    )
    out_specs = (
        P(None, "dp", "tensor", None),
        P(None, "dp", "tensor", None),
        P("dp"),
        P("dp"),
        P("dp", None),
        P("dp", None),
        P("dp", None),
        P("dp", "tensor"),
        P("dp", "tensor"),
        P("dp", None),
        P("tensor", "dp"),
    )
    return jax.shard_map(shards, mesh=mesh, in_specs=in_specs, out_specs=out_specs, check_vma=False)
```

profile of v0, /device:TPU:0, one launch (start us, length us, event | category | flops | bytes accessed | tf_op | source)
XLA Modules:
  0.0 1362.6 jit_solution(11270381272452233820)
XLA Ops:
  14.7 23.7 %all-reduce.5 = (bf16[1152]{0:T(1024)(128)(2,1)S(1)}, bf16[1152]{0:T(1024)(128)(2,1)S(1)}) all-reduce(bf16[1152]{0:T(1024)(128)(2,1)S(1)} %dynamic-update-slice, bf16[1152]{0:T(1024)(128)(2,1)S(1)} %dynamic-update-slice.1), channel_id=1, replica_groups=mesh['dp'=8,'tensor'=4] {'dp'}, use_global_device_ids=true, to_apply=%add | all-reduce | flops 2304 | bytes 9216
  38.8 34.3 %all_gather.61 = bf16[1152,384]{1,0:T(8,128)(2,1)S(1)} all-gather(bf16[144,384]{1,0:T(8,128)(2,1)S(1)} %copy-done.50), channel_id=1, replica_groups=mesh['dp'=8,'tensor'=4] {'dp'}, dimensions={0}, use_global_device_ids=true | all-gather | bytes 995328 | tf_op jit(solution)/shard_map/all_gather | solution.py:58
  74.6 8.8 all_gather.62
  84.6 34.1 %all_gather.63 = bf16[1152,384]{1,0:T(8,128)(2,1)S(1)} all-gather(bf16[144,384]{1,0:T(8,128)(2,1)S(1)} %copy-done.51), channel_id=1, replica_groups=mesh['dp'=8,'tensor'=4] {'dp'}, dimensions={0}, use_global_device_ids=true | all-gather | bytes 995328 | tf_op jit(solution)/shard_map/all_gather | solution.py:57
  121.5 7.5 all_gather.64
  141.4 7.9 fusion.8
  149.4 10.4 exponential_reduce_fusion.1
  159.8 9.5 convolution_convert_fusion.5
  179.3 9.2 all-gather.18.cloned.1.call-done
  188.6 25.0 %all-gather.14.cloned.1.call-done = bf16[1024,1152]{1,0:T(8,128)(2,1)} async-done(((bf16[256,1152]{1,0:T(8,128)(2,1)}), bf16[1024,1152]{1,0:T(8,128)(2,1)}) %all-gather.14.cloned.1.call-update) | async-done | bytes 2359312 | tf_op jit(solution)/shard_map/all_gather | solution.py:196
  213.6 6.1 fusion.138
  219.7 41.9 %all-gather.16.cloned.1.call-done = bf16[1152,768]{1,0:T(8,128)(2,1)} async-done(((bf16[144,768]{1,0:T(8,128)(2,1)}), bf16[1152,768]{1,0:T(8,128)(2,1)}) %all-gather.16.cloned.1.call-update) | async-done | bytes 1769488 | tf_op jit(solution)/shard_map/all_gather | solution.py:59
  261.6 6.0 fusion.137
  267.6 41.0 %all-gather.20.cloned.1.call-done = bf16[768,1152]{0,1:T(8,128)(2,1)} async-done(((bf16[768,144]{0,1:T(8,128)(2,1)}), bf16[768,1152]{0,1:T(8,128)(2,1)}) %all-gather.20.cloned.1.call-update) | async-done | bytes 1769488 | tf_op jit(solution)/shard_map/all_gather | solution.py:62
  308.6 25.3 %all-gather.24.cloned.1.call-done = bf16[1024,1152]{1,0:T(8,128)(2,1)} async-done(((bf16[256,1152]{1,0:T(8,128)(2,1)}), bf16[1024,1152]{1,0:T(8,128)(2,1)}) %all-gather.24.cloned.1.call-update) | async-done | bytes 2359312 | tf_op jit(solution)/shard_map/all_gather | solution.py:268
  333.8 8.4 multiply_convert_fusion.2
  350.3 9.1 all_gather.72
  361.6 12.0 all_gather.73
  373.6 8.0 fusion.9
  381.7 10.8 exponential_reduce_fusion
  393.2 11.0 convolution_convert_fusion.4
  410.5 23.5 %all-gather.22.cloned.1.call-done = bf16[1024,1152]{1,0:T(8,128)(2,1)} async-done(((bf16[256,1152]{1,0:T(8,128)(2,1)}), bf16[1024,1152]{1,0:T(8,128)(2,1)}) %all-gather.22.cloned.1.call-update) | async-done | bytes 2359312 | tf_op jit(solution)/shard_map/all_gather | solution.py:196
  434.0 6.2 fusion.140
  444.0 15.5 %all-gather.26.cloned.1.call-done = bf16[1024,1152]{1,0:T(8,128)(2,1)} async-done(((bf16[256,1152]{1,0:T(8,128)(2,1)}), bf16[1024,1152]{1,0:T(8,128)(2,1)}) %all-gather.26.cloned.1.call-update) | async-done | bytes 2359312 | tf_op jit(solution)/shard_map/all_gather | solution.py:268
  459.6 8.3 multiply_convert_fusion
  474.2 5.6 convolution_convert_fusion.1
  480.3 5.9 convolution_convert_fusion
  487.6 19.8 %reduce-scatter.26.cloned.1.call-done = bf16[256,1152]{1,0:T(8,128)(2,1)} async-done(((bf16[1024,1152]{1,0:T(8,128)(2,1)}), bf16[256,1152]{1,0:T(8,128)(2,1)}) %reduce-scatter.26.cloned.1.call-update) | async-done | bytes 589840 | tf_op jit(solution)/shard_map/reduce_scatter | solution.py:81
  510.0 32.9 %reduce-scatter.16.cloned.1.call-done = bf16[256,1152]{1,0:T(8,128)(2,1)} async-done(((bf16[1024,1152]{1,0:T(8,128)(2,1)}), bf16[256,1152]{1,0:T(8,128)(2,1)}) %reduce-scatter.16.cloned.1.call-update) | async-done | bytes 589840 | tf_op jit(solution)/shard_map/reduce_scatter | solution.py:67
  542.9 35.8 %reduce-scatter.18.cloned.1.call-done = bf16[256,1152]{1,0:T(8,128)(2,1)} async-done(((bf16[1024,1152]{1,0:T(8,128)(2,1)}), bf16[256,1152]{1,0:T(8,128)(2,1)}) %reduce-scatter.18.cloned.1.call-update) | async-done | bytes 589840 | tf_op jit(solution)/shard_map/reduce_scatter | solution.py:67
  593.9 12.0 bitcast_convert_fusion.1
  606.0 12.2 bitcast_convert_fusion
  618.2 12.7 fusion
  631.2 13.6 fusion.2
  652.2 12.8 fusion.3
  665.2 13.6 fusion.5
  689.1 25.8 %reduce-scatter.22.cloned.1.call-done = bf16[256,384]{0,1:T(8,128)(2,1)} async-done(((bf16[1024,384]{0,1:T(8,128)(2,1)}), bf16[256,384]{0,1:T(8,128)(2,1)}) %reduce-scatter.22.cloned.1.call-update) | async-done | bytes 196624 | tf_op jit(solution)/shard_map/reduce_scatter | solution.py:316
  745.3 6.0 fusion.145
  751.3 33.2 %reduce-scatter.36.cloned.1.call-done = f32[144,384]{1,0:T(8,128)} async-done(((f32[1152,384]{1,0:T(8,128)}), f32[144,384]{1,0:T(8,128)}) %reduce-scatter.36.cloned.1.call-update) | async-done | bytes 221200 | tf_op jit(solution)/shard_map/reduce_scatter | solution.py:101
  786.1 67.5 %reduce-scatter.34.cloned.1.call-done = f32[144,384]{1,0:T(8,128)} async-done(((f32[1152,384]{1,0:T(8,128)}), f32[144,384]{1,0:T(8,128)}) %reduce-scatter.34.cloned.1.call-update) | async-done | bytes 221200 | tf_op jit(solution)/shard_map/reduce_scatter | solution.py:100
  855.2 104.9 %reduce-scatter.42.cloned.1.call-done = f32[144,1152]{1,0:T(8,128)} async-done(((f32[1152,1152]{1,0:T(8,128)}), f32[144,1152]{1,0:T(8,128)}) %reduce-scatter.42.cloned.1.call-update) | async-done | bytes 663568 | tf_op jit(solution)/shard_map/reduce_scatter | solution.py:104
  962.0 106.2 %reduce-scatter.32.cloned.1.call-done = f32[144,1152]{1,0:T(8,128)} async-done(((f32[1152,1152]{1,0:T(8,128)}), f32[144,1152]{1,0:T(8,128)}) %reduce-scatter.32.cloned.1.call-update) | async-done | bytes 663568 | tf_op jit(solution)/shard_map/reduce_scatter | solution.py:99
  1070.1 7.0 convolution_add_fusion.4
  1107.6 37.4 %all-reduce.4 = (bf16[1152]{0:T(1024)(128)(2,1)}, bf16[1152]{0:T(1024)(128)(2,1)}) all-reduce(f32[1152]{0:T(1024)} %add.291, f32[1152]{0:T(1024)} %add.292), channel_id=10, replica_groups=mesh['dp'=8,'tensor'=4] {'dp'}, use_global_device_ids=true, to_apply=%region_24.25.clone | all-reduce | flops 2304 | bytes 13824
  1147.5 6.7 all-reduce.6
  1167.3 23.0 %reduce-scatter.38.cloned.1.call-done = f32[144,768]{1,0:T(8,128)} async-done(((f32[1152,768]{1,0:T(8,128)}), f32[144,768]{1,0:T(8,128)}) %reduce-scatter.38.cloned.1.call-update) | async-done | bytes 442384 | tf_op jit(solution)/shard_map/reduce_scatter | solution.py:102
  1190.3 82.8 %reduce-scatter.40.cloned.1.call-done = f32[144,768]{1,0:T(8,128)} async-done(((f32[1152,768]{1,0:T(8,128)}), f32[144,768]{1,0:T(8,128)}) %reduce-scatter.40.cloned.1.call-update) | async-done | bytes 442384 | tf_op jit(solution)/shard_map/reduce_scatter | solution.py:103
  1273.2 82.7 %reduce-scatter.44.cloned.1.call-done = f32[768,144]{0,1:T(8,128)} async-done(((f32[768,1152]{0,1:T(8,128)}), f32[768,144]{0,1:T(8,128)}) %reduce-scatter.44.cloned.1.call-update) | async-done | bytes 442384 | tf_op jit(solution)/shard_map/reduce_scatter | solution.py:105
  (331 shorter events, 182.5 us)
Async XLA Ops:
  7.2 31.6 %copy-start.50 = (bf16[144,384]{1,0:T(8,128)(2,1)S(1)}, bf16[144,384]{1,0:T(8,128)(2,1)}, u32[]{:S(2)}) copy-start(bf16[144,384]{1,0:T(8,128)(2,1)} %param.18) | copy-start | bytes 331780
  7.2 124.0 %all-gather.10.cloned.1.call-start = ((), (), s32[]{:S(2)}) async-start(), calls=%async_computation.15 | async-start | bytes 2985984 | tf_op jit(solution)/shard_map/all_gather | solution.py:56
  8.0 66.0 %copy-start.2 = (bf16[2,1,256,1152]{3,2,1,0:T(8,128)(2,1)S(1)}, bf16[2,1,256,1152]{3,2,1,0:T(8,128)(2,1)}, u32[]{:S(2)}) copy-start(bf16[2,1,256,1152]{3,2,1,0:T(8,128)(2,1)} %param.12) | copy-start | bytes 3538948
  8.0 161.3 %all-gather.12.cloned.1.call-start = ((), (), s32[]{:S(2)}) async-start(), calls=%async_computation.16 | async-start | bytes 2985984 | tf_op jit(solution)/shard_map/all_gather | solution.py:61
  8.7 179.8 %all-gather.18.cloned.1.call-start = ((), (), s32[]{:S(2)}) async-start(), calls=%async_computation.19 | async-start | bytes 1990656 | tf_op jit(solution)/shard_map/all_gather | solution.py:60
  9.5 204.1 %all-gather.14.cloned.1.call-start = ((), (), s32[]{:S(2)}) async-start(), calls=%async_computation.17 | async-start | bytes 2949120 | tf_op jit(solution)/shard_map/all_gather | solution.py:196
  38.5 310.0 %copy-start.46 = (f32[1152]{0:T(1024)}, f32[1152]{0:T(1024)S(1)}, u32[]{:S(2)}) copy-start(f32[1152]{0:T(1024)S(1)} %convert_element_type.339) | copy-start | bytes 13828
  38.7 102.1 %copy-start.28 = (f32[256,64]{0,1:T(8,128)}, f32[256,64]{0,1:T(8,128)S(1)}, u32[]{:S(2)}) copy-start(f32[256,64]{0,1:T(8,128)S(1)} %pad_maximum_fusion.4) | copy-start | bytes 196612
  38.8 102.1 %copy-start.37 = (f32[256,64]{0,1:T(8,128)}, f32[256,64]{0,1:T(8,128)S(1)}, u32[]{:S(2)}) copy-start(f32[256,64]{0,1:T(8,128)S(1)} %pad_maximum_fusion.5) | copy-start | bytes 196612
  73.7 65.7 %copy-start.52 = (f32[256]{0:T(256)}, f32[256]{0:T(256)S(1)}, u32[]{:S(2)}) copy-start(f32[256]{0:T(256)S(1)} %get-tuple-element.144) | copy-start | bytes 3076
  73.7 274.8 %copy-start.54 = (f32[256]{0:T(256)}, f32[256]{0:T(256)S(1)}, u32[]{:S(2)}) copy-start(f32[256]{0:T(256)S(1)} %get-tuple-element.120) | copy-start | bytes 3076
  129.0 12.4 copy-start.12
  172.3 234.0 %copy-start.10 = (f32[256,1152]{1,0:T(8,128)}, f32[256,1152]{1,0:T(8,128)S(1)}, u32[]{:S(2)}) copy-start(f32[256,1152]{1,0:T(8,128)S(1)} %get-tuple-element.134) | copy-start | bytes 3538948
  174.0 87.6 %all-gather.16.cloned.1.call-start = ((), (), s32[]{:S(2)}) async-start(), calls=%async_computation.18 | async-start | bytes 1990656 | tf_op jit(solution)/shard_map/all_gather | solution.py:59
  174.6 134.0 %all-gather.20.cloned.1.call-start = ((), (), s32[]{:S(2)}) async-start(), calls=%async_computation.20 | async-start | bytes 1990656 | tf_op jit(solution)/shard_map/all_gather | solution.py:62
  175.1 158.7 %all-gather.24.cloned.1.call-start = ((), (), s32[]{:S(2)}) async-start(), calls=%async_computation.24 | async-start | bytes 2949120 | tf_op jit(solution)/shard_map/all_gather | solution.py:268
  176.7 43.0 %copy-start.58 = (f32[256]{0:T(256)}, f32[256]{0:T(256)S(1)}, u32[]{:S(2)}) copy-start(f32[256]{0:T(256)S(1)} %get-tuple-element.146) | copy-start | bytes 3076
  176.7 43.0 %copy-start.60 = (f32[256]{0:T(256)}, f32[256]{0:T(256)S(1)}, u32[]{:S(2)}) copy-start(f32[256]{0:T(256)S(1)} %get-tuple-element.147) | copy-start | bytes 3076
  179.3 227.0 %reduce-scatter.20.cloned.1.call-start = ((), (), s32[]{:S(2)}) async-start(), calls=%async_computation.25 | async-start | bytes 2949120 | tf_op jit(solution)/shard_map/reduce_scatter | solution.py:81
  348.5 85.5 %all-gather.22.cloned.1.call-start = ((), (), s32[]{:S(2)}) async-start(), calls=%async_computation.22 | async-start | bytes 2949120 | tf_op jit(solution)/shard_map/all_gather | solution.py:196
  393.2 11.0 copy-start.65
  409.7 49.9 %all-gather.26.cloned.1.call-start = ((), (), s32[]{:S(2)}) async-start(), calls=%async_computation.28 | async-start | bytes 2949120 | tf_op jit(solution)/shard_map/all_gather | solution.py:268
  410.2 97.2 %reduce-scatter.26.cloned.1.call-start = ((), (), s32[]{:S(2)}) async-start(), calls=%async_computation.29 | async-start | bytes 2949120 | tf_op jit(solution)/shard_map/reduce_scatter | solution.py:81
  474.2 68.7 %reduce-scatter.16.cloned.1.call-start = ((), (), s32[]{:S(2)}) async-start(), calls=%async_computation.21 | async-start | bytes 2949120 | tf_op jit(solution)/shard_map/reduce_scatter | solution.py:67
  479.9 98.8 %reduce-scatter.18.cloned.1.call-start = ((), (), s32[]{:S(2)}) async-start(), calls=%async_computation.23 | async-start | bytes 2949120 | tf_op jit(solution)/shard_map/reduce_scatter | solution.py:67
  486.2 21.2 %copy-start.11 = (f32[256,1152]{1,0:T(8,128)S(1)}, f32[256,1152]{1,0:T(8,128)}, u32[]{:S(2)}) copy-start(f32[256,1152]{1,0:T(8,128)} %get-tuple-element.138) | copy-start | bytes 3538948
  486.2 92.5 %copy-start.59 = (f32[256]{0:T(256)S(1)}, f32[256]{0:T(256)}, u32[]{:S(2)}) copy-start(f32[256]{0:T(256)} %copy-done.58) | copy-start | bytes 3076
  486.2 92.5 %copy-start.61 = (f32[256]{0:T(256)S(1)}, f32[256]{0:T(256)}, u32[]{:S(2)}) copy-start(f32[256]{0:T(256)} %copy-done.60) | copy-start | bytes 3076
  486.2 92.5 %copy-start.62 = (f32[256]{0:T(256)S(1)}, f32[256]{0:T(256)}, u32[]{:S(2)}) copy-start(f32[256]{0:T(256)} %get-tuple-element.121) | copy-start | bytes 3076
  486.3 196.6 %reduce-scatter.24.cloned.1.call-start = ((), (), s32[]{:S(2)}) async-start(), calls=%async_computation.27 | async-start | bytes 983040 | tf_op jit(solution)/shard_map/reduce_scatter | solution.py:322
  583.0 136.7 %copy-start.5 = (f32[256,1152]{1,0:T(8,128)}, f32[256,1152]{1,0:T(8,128)S(1)}, u32[]{:S(2)}) copy-start(f32[256,1152]{1,0:T(8,128)S(1)} %get-tuple-element.74) | copy-start | bytes 3538948
  605.9 79.7 %reduce-scatter.30.cloned.1.call-start = ((), (), s32[]{:S(2)}) async-start(), calls=%async_computation.31 | async-start | bytes 983040 | tf_op jit(solution)/shard_map/reduce_scatter | solution.py:322
  606.0 12.2 copy-start.20
  606.0 12.2 copy-start.23
  631.0 58.2 %reduce-scatter.28.cloned.1.call-start = ((), (), s32[]{:S(2)}) async-start(), calls=%async_computation.30 | async-start | bytes 983040 | tf_op jit(solution)/shard_map/reduce_scatter | solution.py:316
  665.1 49.8 %reduce-scatter.22.cloned.1.call-start = ((), (), s32[]{:S(2)}) async-start(), calls=%async_computation.26 | async-start | bytes 983040 | tf_op jit(solution)/shard_map/reduce_scatter | solution.py:316
  665.2 13.6 copy-start.17
  682.8 101.7 %reduce-scatter.36.cloned.1.call-start = ((), (), s32[]{:S(2)}) async-start(), calls=%async_computation.34 | async-start | bytes 1990656 | tf_op jit(solution)/shard_map/reduce_scatter | solution.py:101
  689.0 25.9 %copy-start.38 = (f32[256,64]{0,1:T(8,128)S(1)}, f32[256,64]{0,1:T(8,128)}, u32[]{:S(2)}) copy-start(f32[256,64]{0,1:T(8,128)} %copy-done.37) | copy-start | bytes 196612
  689.1 164.5 %reduce-scatter.34.cloned.1.call-start = ((), (), s32[]{:S(2)}) async-start(), calls=%async_computation.33 | async-start | bytes 1990656 | tf_op jit(solution)/shard_map/reduce_scatter | solution.py:100
  719.6 240.5 %reduce-scatter.42.cloned.1.call-start = ((), (), s32[]{:S(2)}) async-start(), calls=%async_computation.37 | async-start | bytes 5971968 | tf_op jit(solution)/shard_map/reduce_scatter | solution.py:104
  725.4 342.8 %reduce-scatter.32.cloned.1.call-start = ((), (), s32[]{:S(2)}) async-start(), calls=%async_computation.32 | async-start | bytes 5971968 | tf_op jit(solution)/shard_map/reduce_scatter | solution.py:99
  745.3 416.1 %all-reduce.10.cloned.1.call-start = ((), (), s32[]{:S(2)}) async-start(), calls=%async_computation.39 | async-start | bytes 1769472 | tf_op jit(solution)/shard_map/psum | solution.py:408
  1070.0 120.3 %reduce-scatter.38.cloned.1.call-start = ((), (), s32[]{:S(2)}) async-start(), calls=%async_computation.35 | async-start | bytes 3981312 | tf_op jit(solution)/shard_map/reduce_scatter | solution.py:102
  1077.1 196.0 %reduce-scatter.40.cloned.1.call-start = ((), (), s32[]{:S(2)}) async-start(), calls=%async_computation.36 | async-start | bytes 3981312 | tf_op jit(solution)/shard_map/reduce_scatter | solution.py:103
  1085.6 270.2 %reduce-scatter.44.cloned.1.call-start = ((), (), s32[]{:S(2)}) async-start(), calls=%async_computation.38 | async-start | bytes 3981312 | tf_op jit(solution)/shard_map/reduce_scatter | solution.py:105
  1104.6 53.3 %copy-start.6 = (f32[256,1152]{1,0:T(8,128)S(1)}, f32[256,1152]{1,0:T(8,128)}, u32[]{:S(2)}) copy-start(f32[256,1152]{1,0:T(8,128)} %copy-done.5) | copy-start | bytes 3538948
  1104.6 53.3 %copy-start.9 = (f32[256,1152]{1,0:T(8,128)S(1)}, f32[256,1152]{1,0:T(8,128)}, u32[]{:S(2)}) copy-start(f32[256,1152]{1,0:T(8,128)} %copy-done.7) | copy-start | bytes 3538948
  (60 other events, 221.8 us)
Sparse Core Ops, SparseCore 0:
  10.2 70.2 all-gather.9
  82.7 58.9 all-gather.11
  143.9 44.6 all-gather.17
  190.6 22.9 all-gather.13
  215.6 45.9 all-gather.15
  263.6 44.9 all-gather.19
  310.7 23.0 all-gather.23
  348.6 35.2 reduce-scatter.19
  409.8 24.1 all-gather.21
  435.4 24.0 all-gather.25
  474.3 33.0 reduce-scatter.25
  509.8 33.0 reduce-scatter.15
  545.6 33.0 reduce-scatter.17
  606.0 23.2 reduce-scatter.23
  631.9 23.2 reduce-scatter.29
  665.2 23.2 reduce-scatter.27
  691.6 23.2 reduce-scatter.21
  718.2 66.2 reduce-scatter.35
  788.4 65.1 reduce-scatter.33
  857.0 103.0 reduce-scatter.41
  964.2 103.9 reduce-scatter.31
  1071.3 35.1 all-reduce.9
  1110.7 79.6 reduce-scatter.37
  1194.4 78.7 reduce-scatter.39
  1277.4 78.4 reduce-scatter.43
where the time goes:
time: 1370 us; the launch traced here: 1360 us
  waiting for transfers between devices  800 us (58%)
  matrix products  238 us (17%)
  blocking collectives  173 us (13%)
  other arithmetic  102 us (7%)
  local copies, waits for them, and re-layouts  30.1 us (2%)
  between operations  16.6 us (1%)
    reduce_scatter x1, waiting for transfers between devices, reduce_over_data(): lax.psum_scatter(grad_query_w, 'dp', scatter_dimension=0, tiled=True)  106 us
    reduce_scatter x1, waiting for transfers between devices, reduce_over_data(): lax.psum_scatter(grad_out_w, 'dp', scatter_dimension=0, tiled=True)  105 us
    reduce_scatter x1, waiting for transfers between devices, reduce_over_data(): lax.psum_scatter(grad_up_w, 'dp', scatter_dimension=0, tiled=True)  82.8 us
    reduce_scatter x1, waiting for transfers between devices, reduce_over_data(): lax.psum_scatter(grad_down_w, 'dp', scatter_dimension=1, tiled=True)  82.7 us
    reduce_scatter x2, waiting for transfers between devices, project_sum(): lax.psum_scatter(jnp.dot(left_side, right_side, preferred_element_type=jn...  68.7 us
    reduce_scatter x1, waiting for transfers between devices, reduce_over_data(): lax.psum_scatter(grad_key_w, 'dp', scatter_dimension=0, tiled=True)  67.5 us
    unnamed x2, blocking collectives  61.1 us
    all_gather x2, waiting for transfers between devices, forward_pass(): lax.all_gather((middle * scale_two * gain_two).astype(jnp.bfloat16), 'ten...  48.5 us
  transfers between devices with their start and end apart: 25, of which 18 were waited for; matrix products, arithmetic and copies ran while one was open for 22% of the time, Pallas kernels for 0%

commit v1 on v0

--- a/solution.py
+++ b/solution.py
@@ -7,6 +7,22 @@
 EPSILON = 1e-05
 ROPE_BASE = 10000.0
 MASKED = -1e30
+
+
+def ring_gather(x, axis, dim):
+    ways, here, turn = (lax.axis_size(axis), lax.axis_index(axis), x.shape[dim])
+    shape = [n * ways if d == dim else n for d, n in enumerate(x.shape)]
+    full = lax.dynamic_update_slice_in_dim(jnp.zeros(shape, x.dtype), x, here * turn, axis=dim)
+    going_up = going_down = x
+    for far in range(1, ways // 2 + 1):
+        going_up = lax.ppermute(going_up, axis, [(d, (d + 1) % ways) for d in range(ways)])
+        full = lax.dynamic_update_slice_in_dim(full, going_up, (here - far) % ways * turn, axis=dim)
+        if 2 * far < ways:
+            going_down = lax.ppermute(going_down, axis, [(d, (d - 1) % ways) for d in range(ways)])
+            full = lax.dynamic_update_slice_in_dim(
+                full, going_down, (here + far) % ways * turn, axis=dim
+            )
+    return full
 
 
 def rope_tables(positions, head_dim):
@@ -59,7 +75,7 @@
         lax.all_gather(w_gate, "dp", axis=0, tiled=True),
         lax.all_gather(w_up, "dp", axis=0, tiled=True),
         lax.all_gather(w_out, "dp", axis=0, tiled=True),
-        lax.all_gather(w_down, "dp", axis=1, tiled=True),
+        ring_gather(w_down, "dp", 1),
     )
 
 

time: 1370 us -> 1330 us (0.971)
  waiting for transfers between devices: 800 us -> 735 us
  starting transfers between devices: 2.57 us -> 17.4 us
    all_gather x1 -> x0, waiting for transfers between devices: 41 us -> none  [fetch_weights(): lax.all_gather(w_down, 'dp', axis=1, tiled=True)]
    all_gather x2, waiting for transfers between devices: 48.5 us -> 23.3 us  [forward_pass(): lax.all_gather((middle * scale_two * gain_two).astype(jnp.bfloat16), 'ten...]
    ppermute x0 -> x7, waiting for transfers between devices: none -> 23.5 us  [the longest x4 15 us: ring_gather(): lax.ppermute(going_up, axis, [(d, (d + 1) % ways) for d in range(ways)])]
    ppermute x0 -> x7, starting transfers between devices: none -> 14.9 us  [the longest x3 11.8 us: ring_gather(): lax.ppermute(going_down, axis, [(d, (d - 1) % ways) for d in range(ways)])]
  transfers between devices with their start and end apart: 25 -> 31, of which waited for: 18 -> 20; matrix products, arithmetic and copies ran while one was open for 22% -> 23% of each run, Pallas kernels for 0% -> 0%
where the time goes in v1:
time: 1330 us; the launch traced here: 1320 us
  waiting for transfers between devices  735 us (55%)
  matrix products  238 us (18%)
  blocking collectives  174 us (13%)
  other arithmetic  102 us (8%)
  local copies, waits for them, and re-layouts  39.1 us (3%)
  starting transfers between devices  17.4 us (1%)
  between operations  17 us (1%)
    reduce_scatter x1, waiting for transfers between devices, reduce_over_data(): lax.psum_scatter(grad_query_w, 'dp', scatter_dimension=0, tiled=True)  106 us
    reduce_scatter x1, waiting for transfers between devices, reduce_over_data(): lax.psum_scatter(grad_out_w, 'dp', scatter_dimension=0, tiled=True)  105 us
    reduce_scatter x1, waiting for transfers between devices, reduce_over_data(): lax.psum_scatter(grad_down_w, 'dp', scatter_dimension=1, tiled=True)  82.7 us
    reduce_scatter x1, waiting for transfers between devices, reduce_over_data(): lax.psum_scatter(grad_up_w, 'dp', scatter_dimension=0, tiled=True)  82.7 us
    reduce_scatter x2, waiting for transfers between devices, project_sum(): lax.psum_scatter(jnp.dot(left_side, right_side, preferred_element_type=jn...  68.7 us
    reduce_scatter x1, waiting for transfers between devices, reduce_over_data(): lax.psum_scatter(grad_key_w, 'dp', scatter_dimension=0, tiled=True)  67.3 us
    unnamed x2, blocking collectives  61 us
    dot_general x14, matrix products, contract_rows(): lax.dot_general(left_side, right_side, (((0,), (0,)), ((), ())), preferre...  46.9 us
  transfers between devices with their start and end apart: 31, of which 20 were waited for; matrix products, arithmetic and copies ran while one was open for 23% of the time, Pallas kernels for 0%

profile of v1, /device:TPU:0, one launch (start us, length us, event | category | flops | bytes accessed | tf_op | source)
XLA Modules:
  0.0 1321.5 jit_solution(9649227401611040573)
XLA Ops:
  14.8 23.7 %all-reduce.5 = (bf16[1152]{0:T(1024)(128)(2,1)S(1)}, bf16[1152]{0:T(1024)(128)(2,1)S(1)}) all-reduce(bf16[1152]{0:T(1024)(128)(2,1)S(1)} %dynamic-update-slice, bf16[1152]{0:T(1024)(128)(2,1)S(1)} %dynamic-update-slice.1), channel_id=1, replica_groups=mesh['dp'=8,'tensor'=4] {'dp'}, use_global_device_ids=true, to_apply=%add | all-reduce | flops 2304 | bytes 9216
  38.8 34.4 %all_gather.57 = bf16[1152,384]{1,0:T(8,128)(2,1)S(1)} all-gather(bf16[144,384]{1,0:T(8,128)(2,1)S(1)} %copy-done.51), channel_id=1, replica_groups=mesh['dp'=8,'tensor'=4] {'dp'}, dimensions={0}, use_global_device_ids=true | all-gather | bytes 995328 | tf_op jit(solution)/shard_map/all_gather | solution.py:74
  74.7 8.8 all_gather.58
  84.8 34.3 %all_gather.59 = bf16[1152,384]{1,0:T(8,128)(2,1)S(1)} all-gather(bf16[144,384]{1,0:T(8,128)(2,1)S(1)} %copy-done.52), channel_id=1, replica_groups=mesh['dp'=8,'tensor'=4] {'dp'}, dimensions={0}, use_global_device_ids=true | all-gather | bytes 995328 | tf_op jit(solution)/shard_map/all_gather | solution.py:73
  121.9 7.3 all_gather.60
  141.7 7.9 fusion.8
  149.6 10.3 exponential_reduce_fusion.1
  160.0 9.5 convolution_convert_fusion.5
  183.2 7.4 collective-permute-done.1
  210.9 5.9 collective-permute-done.4
  218.2 7.4 collective-permute-done.6
  226.3 6.1 fusion.138
  232.4 35.7 %all-gather.15.cloned.1.call-done = bf16[1152,768]{1,0:T(8,128)(2,1)} async-done(((bf16[144,768]{1,0:T(8,128)(2,1)}), bf16[1152,768]{1,0:T(8,128)(2,1)}) %all-gather.15.cloned.1.call-update) | async-done | bytes 1769488 | tf_op jit(solution)/shard_map/all_gather | solution.py:75
  268.1 6.1 fusion.137
  274.1 19.0 %all-gather.21.cloned.1.call-done = bf16[1024,1152]{1,0:T(8,128)(2,1)} async-done(((bf16[256,1152]{1,0:T(8,128)(2,1)}), bf16[1024,1152]{1,0:T(8,128)(2,1)}) %all-gather.21.cloned.1.call-update) | async-done | bytes 2359312 | tf_op jit(solution)/shard_map/all_gather | solution.py:284
  293.2 8.4 multiply_convert_fusion.2
  309.6 9.1 all_gather.67
  321.0 12.0 all_gather.68
  332.9 8.0 fusion.9
  340.9 10.8 exponential_reduce_fusion
  352.5 11.0 convolution_convert_fusion.4
  369.9 23.3 %all-gather.19.cloned.1.call-done = bf16[1024,1152]{1,0:T(8,128)(2,1)} async-done(((bf16[256,1152]{1,0:T(8,128)(2,1)}), bf16[1024,1152]{1,0:T(8,128)(2,1)}) %all-gather.19.cloned.1.call-update) | async-done | bytes 2359312 | tf_op jit(solution)/shard_map/all_gather | solution.py:212
  393.2 6.2 fusion.140
  403.2 15.7 %all-gather.23.cloned.1.call-done = bf16[1024,1152]{1,0:T(8,128)(2,1)} async-done(((bf16[256,1152]{1,0:T(8,128)(2,1)}), bf16[1024,1152]{1,0:T(8,128)(2,1)}) %all-gather.23.cloned.1.call-update) | async-done | bytes 2359312 | tf_op jit(solution)/shard_map/all_gather | solution.py:284
  419.0 8.4 multiply_convert_fusion
  433.6 5.6 convolution_convert_fusion.1
  439.7 5.9 convolution_convert_fusion
  447.1 19.7 %reduce-scatter.26.cloned.1.call-done = bf16[256,1152]{1,0:T(8,128)(2,1)} async-done(((bf16[1024,1152]{1,0:T(8,128)(2,1)}), bf16[256,1152]{1,0:T(8,128)(2,1)}) %reduce-scatter.26.cloned.1.call-update) | async-done | bytes 589840 | tf_op jit(solution)/shard_map/reduce_scatter | solution.py:97
  469.4 33.1 %reduce-scatter.16.cloned.1.call-done = bf16[256,1152]{1,0:T(8,128)(2,1)} async-done(((bf16[1024,1152]{1,0:T(8,128)(2,1)}), bf16[256,1152]{1,0:T(8,128)(2,1)}) %reduce-scatter.16.cloned.1.call-update) | async-done | bytes 589840 | tf_op jit(solution)/shard_map/reduce_scatter | solution.py:83
  502.4 35.6 %reduce-scatter.18.cloned.1.call-done = bf16[256,1152]{1,0:T(8,128)(2,1)} async-done(((bf16[1024,1152]{1,0:T(8,128)(2,1)}), bf16[256,1152]{1,0:T(8,128)(2,1)}) %reduce-scatter.18.cloned.1.call-update) | async-done | bytes 589840 | tf_op jit(solution)/shard_map/reduce_scatter | solution.py:83
  553.2 12.0 bitcast_convert_fusion.1
  565.3 12.2 bitcast_convert_fusion
  577.5 12.7 fusion
  590.5 13.6 %fusion.2 = bf16[6,3,256,1024]{2,3,1,0:T(8,128)(2,1)S(1)} fusion(f32[6,1024,256,3]{2,1,3,0:T(8,128)} %get-tuple-element.142, f32[6,1024,256,3]{2,1,3,0:T(8,128)} %get-tuple-element.136, f32[6,3,256]{2,1,0:T(4,128)S(1)} %get-tuple-element.141, f32[6,3,256]{2,1,0:T(4,128)S(1)} %log_add_fusion, pred[256,1024]{0,1:T(8,128)(4,1)S(1)} %get-tuple-element.126), kind=kLoop, calls=%fused_computation.4 | loop fusion | flops 28311552 | bytes 47484928 | tf_op jit(solution)/shard_map/convert_element_type | solution.py:310
  611.5 12.8 fusion.3
  624.4 13.6 %fusion.5 = bf16[6,3,256,1024]{2,3,1,0:T(8,128)(2,1)S(1)} fusion(f32[6,1024,256,3]{2,1,3,0:T(8,128)} %get-tuple-element.140, f32[6,1024,256,3]{2,1,3,0:T(8,128)} %get-tuple-element.132, f32[6,3,256]{2,1,0:T(4,128)S(1)} %get-tuple-element.139, f32[6,3,256]{2,1,0:T(4,128)S(1)} %log_add_fusion.1, pred[256,1024]{0,1:T(8,128)(4,1)S(1)} %get-tuple-element.125), kind=kLoop, calls=%fused_computation.9 | loop fusion | flops 28311552 | bytes 47484928 | tf_op jit(solution)/shard_map/convert_element_type | solution.py:310
  648.3 25.8 %reduce-scatter.22.cloned.1.call-done = bf16[256,384]{0,1:T(8,128)(2,1)} async-done(((bf16[1024,384]{0,1:T(8,128)(2,1)}), bf16[256,384]{0,1:T(8,128)(2,1)}) %reduce-scatter.22.cloned.1.call-update) | async-done | bytes 196624 | tf_op jit(solution)/shard_map/reduce_scatter | solution.py:332
  704.6 6.0 fusion.145
  710.6 32.8 %reduce-scatter.36.cloned.1.call-done = f32[144,384]{1,0:T(8,128)} async-done(((f32[1152,384]{1,0:T(8,128)}), f32[144,384]{1,0:T(8,128)}) %reduce-scatter.36.cloned.1.call-update) | async-done | bytes 221200 | tf_op jit(solution)/shard_map/reduce_scatter | solution.py:117
  745.0 67.3 %reduce-scatter.34.cloned.1.call-done = f32[144,384]{1,0:T(8,128)} async-done(((f32[1152,384]{1,0:T(8,128)}), f32[144,384]{1,0:T(8,128)}) %reduce-scatter.34.cloned.1.call-update) | async-done | bytes 221200 | tf_op jit(solution)/shard_map/reduce_scatter | solution.py:116
  813.8 105.1 %reduce-scatter.42.cloned.1.call-done = f32[144,1152]{1,0:T(8,128)} async-done(((f32[1152,1152]{1,0:T(8,128)}), f32[144,1152]{1,0:T(8,128)}) %reduce-scatter.42.cloned.1.call-update) | async-done | bytes 663568 | tf_op jit(solution)/shard_map/reduce_scatter | solution.py:120
  920.8 106.0 %reduce-scatter.32.cloned.1.call-done = f32[144,1152]{1,0:T(8,128)} async-done(((f32[1152,1152]{1,0:T(8,128)}), f32[144,1152]{1,0:T(8,128)}) %reduce-scatter.32.cloned.1.call-update) | async-done | bytes 663568 | tf_op jit(solution)/shard_map/reduce_scatter | solution.py:115
  1028.7 7.0 convolution_add_fusion.4
  1066.3 37.3 %all-reduce.4 = (bf16[1152]{0:T(1024)(128)(2,1)}, bf16[1152]{0:T(1024)(128)(2,1)}) all-reduce(f32[1152]{0:T(1024)} %add.386, f32[1152]{0:T(1024)} %add.387), channel_id=10, replica_groups=mesh['dp'=8,'tensor'=4] {'dp'}, use_global_device_ids=true, to_apply=%region_24.25.clone | all-reduce | flops 2304 | bytes 13824
  1106.2 6.7 all-reduce.6
  1126.0 23.1 %reduce-scatter.38.cloned.1.call-done = f32[144,768]{1,0:T(8,128)} async-done(((f32[1152,768]{1,0:T(8,128)}), f32[144,768]{1,0:T(8,128)}) %reduce-scatter.38.cloned.1.call-update) | async-done | bytes 442384 | tf_op jit(solution)/shard_map/reduce_scatter | solution.py:118
  1149.1 82.7 %reduce-scatter.40.cloned.1.call-done = f32[144,768]{1,0:T(8,128)} async-done(((f32[1152,768]{1,0:T(8,128)}), f32[144,768]{1,0:T(8,128)}) %reduce-scatter.40.cloned.1.call-update) | async-done | bytes 442384 | tf_op jit(solution)/shard_map/reduce_scatter | solution.py:119
  1231.8 82.7 %reduce-scatter.44.cloned.1.call-done = f32[768,144]{0,1:T(8,128)} async-done(((f32[768,1152]{0,1:T(8,128)}), f32[768,144]{0,1:T(8,128)}) %reduce-scatter.44.cloned.1.call-update) | async-done | bytes 442384 | tf_op jit(solution)/shard_map/reduce_scatter | solution.py:121
  (353 shorter events, 208.7 us)
Async XLA Ops:
  7.2 67.0 %copy-start.2 = (bf16[2,1,256,1152]{3,2,1,0:T(8,128)(2,1)S(1)}, bf16[2,1,256,1152]{3,2,1,0:T(8,128)(2,1)}, u32[]{:S(2)}) copy-start(bf16[2,1,256,1152]{3,2,1,0:T(8,128)(2,1)} %param.12) | copy-start | bytes 3538948
  7.2 31.6 %copy-start.51 = (bf16[144,384]{1,0:T(8,128)(2,1)S(1)}, bf16[144,384]{1,0:T(8,128)(2,1)}, u32[]{:S(2)}) copy-start(bf16[144,384]{1,0:T(8,128)(2,1)} %param.18) | copy-start | bytes 331780
  7.2 124.3 %all-gather.9.cloned.1.call-start = ((), (), s32[]{:S(2)}) async-start(), calls=%async_computation.15 | async-start | bytes 2985984 | tf_op jit(solution)/shard_map/all_gather | solution.py:72
  8.0 161.5 %all-gather.11.cloned.1.call-start = ((), (), s32[]{:S(2)}) async-start(), calls=%async_computation.16 | async-start | bytes 2985984 | tf_op jit(solution)/shard_map/all_gather | solution.py:77
  8.7 217.5 %all-gather.17.cloned.1.call-start = ((), (), s32[]{:S(2)}) async-start(), calls=%async_computation.19 | async-start | bytes 1990656 | tf_op jit(solution)/shard_map/all_gather | solution.py:76
  9.5 216.8 %all-gather.13.cloned.1.call-start = ((), (), s32[]{:S(2)}) async-start(), calls=%async_computation.17 | async-start | bytes 2949120 | tf_op jit(solution)/shard_map/all_gather | solution.py:212
  38.5 269.3 %copy-start.46 = (f32[1152]{0:T(1024)}, f32[1152]{0:T(1024)S(1)}, u32[]{:S(2)}) copy-start(f32[1152]{0:T(1024)S(1)} %convert_element_type.339) | copy-start | bytes 13828
  38.8 102.3 %copy-start.28 = (f32[256,64]{0,1:T(8,128)}, f32[256,64]{0,1:T(8,128)S(1)}, u32[]{:S(2)}) copy-start(f32[256,64]{0,1:T(8,128)S(1)} %pad_maximum_fusion.4) | copy-start | bytes 196612
  38.8 102.2 %copy-start.37 = (f32[256,64]{0,1:T(8,128)}, f32[256,64]{0,1:T(8,128)S(1)}, u32[]{:S(2)}) copy-start(f32[256,64]{0,1:T(8,128)S(1)} %pad_maximum_fusion.5) | copy-start | bytes 196612
  73.9 65.8 %copy-start.53 = (f32[256]{0:T(256)}, f32[256]{0:T(256)S(1)}, u32[]{:S(2)}) copy-start(f32[256]{0:T(256)S(1)} %get-tuple-element.144) | copy-start | bytes 3076
  73.9 234.0 %copy-start.55 = (f32[256]{0:T(256)}, f32[256]{0:T(256)S(1)}, u32[]{:S(2)}) copy-start(f32[256]{0:T(256)S(1)} %get-tuple-element.120) | copy-start | bytes 3076
  172.6 193.0 %copy-start.10 = (f32[256,1152]{1,0:T(8,128)}, f32[256,1152]{1,0:T(8,128)S(1)}, u32[]{:S(2)}) copy-start(f32[256,1152]{1,0:T(8,128)S(1)} %get-tuple-element.134) | copy-start | bytes 3538948
  174.2 93.8 %all-gather.15.cloned.1.call-start = ((), (), s32[]{:S(2)}) async-start(), calls=%async_computation.18 | async-start | bytes 1990656 | tf_op jit(solution)/shard_map/all_gather | solution.py:75
  174.8 118.4 %all-gather.21.cloned.1.call-start = ((), (), s32[]{:S(2)}) async-start(), calls=%async_computation.23 | async-start | bytes 2949120 | tf_op jit(solution)/shard_map/all_gather | solution.py:284
  178.9 186.6 %reduce-scatter.20.cloned.1.call-start = ((), (), s32[]{:S(2)}) async-start(), calls=%async_computation.24 | async-start | bytes 2949120 | tf_op jit(solution)/shard_map/reduce_scatter | solution.py:97
  179.0 11.5 collective-permute-start.1
  180.4 15.4 %collective-permute-start = (bf16[768,144]{0,1:T(8,128)(2,1)}, bf16[768,144]{0,1:T(8,128)(2,1)}, u32[]{:S(2)}, u32[]{:S(2)}) collective-permute-start(bf16[768,144]{0,1:T(8,128)(2,1)} %param.22), channel_id=1, source_target_pairs={{0,4},{4,8},{8,12},{12,16},{16,20},{20,24},{24,28},{28,0},{1,5},{5... | collective-permute-start | bytes 663560 | tf_op jit(solution)/shard_map/ppermute | solution.py:18
  190.5 9.6 collective-permute-start.3
  195.8 11.4 collective-permute-start.2
  200.2 17.3 %collective-permute-start.5 = (bf16[768,144]{0,1:T(8,128)(2,1)S(1)}, bf16[768,144]{0,1:T(8,128)(2,1)S(1)}, u32[]{:S(2)}, u32[]{:S(2)}) collective-permute-start(bf16[768,144]{0,1:T(8,128)(2,1)S(1)} %collective-permute-done.3), channel_id=1, source_target_pairs={{0,28},{4,0},{8,4},{12,8},{16,12},{20,16},{24,20},{28,24},{1,29},{... | collective-permute-start | bytes 663560 | tf_op jit(solution)/shard_map/ppermute | solution.py:21
  207.1 9.7 collective-permute-start.4
  216.8 8.8 collective-permute-start.6
  307.8 85.4 %all-gather.19.cloned.1.call-start = ((), (), s32[]{:S(2)}) async-start(), calls=%async_computation.21 | async-start | bytes 2949120 | tf_op jit(solution)/shard_map/all_gather | solution.py:212
  368.9 50.0 %all-gather.23.cloned.1.call-start = ((), (), s32[]{:S(2)}) async-start(), calls=%async_computation.27 | async-start | bytes 2949120 | tf_op jit(solution)/shard_map/all_gather | solution.py:284
  369.7 97.1 %reduce-scatter.26.cloned.1.call-start = ((), (), s32[]{:S(2)}) async-start(), calls=%async_computation.28 | async-start | bytes 2949120 | tf_op jit(solution)/shard_map/reduce_scatter | solution.py:97
  433.6 68.8 %reduce-scatter.16.cloned.1.call-start = ((), (), s32[]{:S(2)}) async-start(), calls=%async_computation.20 | async-start | bytes 2949120 | tf_op jit(solution)/shard_map/reduce_scatter | solution.py:83
  439.3 98.8 %reduce-scatter.18.cloned.1.call-start = ((), (), s32[]{:S(2)}) async-start(), calls=%async_computation.22 | async-start | bytes 2949120 | tf_op jit(solution)/shard_map/reduce_scatter | solution.py:83
  445.7 21.1 %copy-start.11 = (f32[256,1152]{1,0:T(8,128)S(1)}, f32[256,1152]{1,0:T(8,128)}, u32[]{:S(2)}) copy-start(f32[256,1152]{1,0:T(8,128)} %get-tuple-element.138) | copy-start | bytes 3538948
  445.7 92.4 %copy-start.60 = (f32[256]{0:T(256)S(1)}, f32[256]{0:T(256)}, u32[]{:S(2)}) copy-start(f32[256]{0:T(256)} %copy-done.59) | copy-start | bytes 3076
  445.7 92.4 %copy-start.62 = (f32[256]{0:T(256)S(1)}, f32[256]{0:T(256)}, u32[]{:S(2)}) copy-start(f32[256]{0:T(256)} %copy-done.61) | copy-start | bytes 3076
  445.7 92.4 %copy-start.63 = (f32[256]{0:T(256)S(1)}, f32[256]{0:T(256)}, u32[]{:S(2)}) copy-start(f32[256]{0:T(256)} %get-tuple-element.121) | copy-start | bytes 3076
  445.7 196.4 %reduce-scatter.24.cloned.1.call-start = ((), (), s32[]{:S(2)}) async-start(), calls=%async_computation.26 | async-start | bytes 983040 | tf_op jit(solution)/shard_map/reduce_scatter | solution.py:338
  542.3 136.6 %copy-start.5 = (f32[256,1152]{1,0:T(8,128)}, f32[256,1152]{1,0:T(8,128)S(1)}, u32[]{:S(2)}) copy-start(f32[256,1152]{1,0:T(8,128)S(1)} %get-tuple-element.74) | copy-start | bytes 3538948
  565.2 79.6 %reduce-scatter.30.cloned.1.call-start = ((), (), s32[]{:S(2)}) async-start(), calls=%async_computation.30 | async-start | bytes 983040 | tf_op jit(solution)/shard_map/reduce_scatter | solution.py:338
  590.2 58.1 %reduce-scatter.28.cloned.1.call-start = ((), (), s32[]{:S(2)}) async-start(), calls=%async_computation.29 | async-start | bytes 983040 | tf_op jit(solution)/shard_map/reduce_scatter | solution.py:332
  624.3 49.8 %reduce-scatter.22.cloned.1.call-start = ((), (), s32[]{:S(2)}) async-start(), calls=%async_computation.25 | async-start | bytes 983040 | tf_op jit(solution)/shard_map/reduce_scatter | solution.py:332
  624.4 13.6 %copy-start.17 = (bf16[256,18,64]{0,2,1:T(8,128)(2,1)S(1)}, bf16[256,18,64]{0,2,1:T(8,128)(2,1)}, u32[]{:S(2)}) copy-start(bf16[256,18,64]{0,2,1:T(8,128)(2,1)} %copy-done.16) | copy-start | bytes 1769476
  642.0 101.4 %reduce-scatter.36.cloned.1.call-start = ((), (), s32[]{:S(2)}) async-start(), calls=%async_computation.33 | async-start | bytes 1990656 | tf_op jit(solution)/shard_map/reduce_scatter | solution.py:117
  648.2 25.9 %copy-start.38 = (f32[256,64]{0,1:T(8,128)S(1)}, f32[256,64]{0,1:T(8,128)}, u32[]{:S(2)}) copy-start(f32[256,64]{0,1:T(8,128)} %copy-done.37) | copy-start | bytes 196612
  648.3 164.0 %reduce-scatter.34.cloned.1.call-start = ((), (), s32[]{:S(2)}) async-start(), calls=%async_computation.32 | async-start | bytes 1990656 | tf_op jit(solution)/shard_map/reduce_scatter | solution.py:116
  678.9 240.1 %reduce-scatter.42.cloned.1.call-start = ((), (), s32[]{:S(2)}) async-start(), calls=%async_computation.36 | async-start | bytes 5971968 | tf_op jit(solution)/shard_map/reduce_scatter | solution.py:120
  684.6 342.2 %reduce-scatter.32.cloned.1.call-start = ((), (), s32[]{:S(2)}) async-start(), calls=%async_computation.31 | async-start | bytes 5971968 | tf_op jit(solution)/shard_map/reduce_scatter | solution.py:115
  704.5 415.5 %all-reduce.10.cloned.1.call-start = ((), (), s32[]{:S(2)}) async-start(), calls=%async_computation.38 | async-start | bytes 1769472 | tf_op jit(solution)/shard_map/psum | solution.py:424
  1028.7 120.4 %reduce-scatter.38.cloned.1.call-start = ((), (), s32[]{:S(2)}) async-start(), calls=%async_computation.34 | async-start | bytes 3981312 | tf_op jit(solution)/shard_map/reduce_scatter | solution.py:118
  1035.8 196.0 %reduce-scatter.40.cloned.1.call-start = ((), (), s32[]{:S(2)}) async-start(), calls=%async_computation.35 | async-start | bytes 3981312 | tf_op jit(solution)/shard_map/reduce_scatter | solution.py:119
  1044.3 270.2 %reduce-scatter.44.cloned.1.call-start = ((), (), s32[]{:S(2)}) async-start(), calls=%async_computation.37 | async-start | bytes 3981312 | tf_op jit(solution)/shard_map/reduce_scatter | solution.py:121
  1063.4 53.1 %copy-start.6 = (f32[256,1152]{1,0:T(8,128)S(1)}, f32[256,1152]{1,0:T(8,128)}, u32[]{:S(2)}) copy-start(f32[256,1152]{1,0:T(8,128)} %copy-done.5) | copy-start | bytes 3538948
  1063.4 53.1 %copy-start.9 = (f32[256,1152]{1,0:T(8,128)S(1)}, f32[256,1152]{1,0:T(8,128)}, u32[]{:S(2)}) copy-start(f32[256,1152]{1,0:T(8,128)} %copy-done.7) | copy-start | bytes 3538948
  (67 other events, 282.6 us)
Sparse Core Ops, SparseCore 0:
  10.2 70.4 all-gather.8
  82.9 58.9 all-gather.10
  144.1 53.8 all-gather.16
  200.0 20.0 all-gather.12
  222.1 45.9 all-gather.14
  270.0 23.0 all-gather.20
  307.9 35.1 reduce-scatter.19
  369.0 24.1 all-gather.18
  394.8 24.0 all-gather.22
  433.7 33.0 reduce-scatter.25
  469.3 33.0 reduce-scatter.15
  505.0 33.0 reduce-scatter.17
  565.3 23.2 reduce-scatter.23
  591.1 23.2 reduce-scatter.29
  624.4 23.2 reduce-scatter.27
  650.9 23.2 reduce-scatter.21
  677.5 65.8 reduce-scatter.35
  747.1 65.0 reduce-scatter.33
  815.8 103.0 reduce-scatter.41
  922.8 103.9 reduce-scatter.31
  1030.0 35.1 all-reduce.9
  1069.4 79.6 reduce-scatter.37
  1153.3 78.4 reduce-scatter.39
  1235.8 78.6 reduce-scatter.43
